TPU v7x, 32 devices: a whole 2x2x4 slice. The times are simulated.
32 devices in a mesh: fibre: 2 (over y), chan: 8 (over z, core), tm: 2 (over x).
Axes of the slice: x: 2, y: 2, z: 4, core: 2. Of those that a mesh axis runs over, the one named last changes fastest.
Arguments:
- raw_strain: bfloat16 [2, 2560, 512], P('tm', 'fibre', 'chan'), parts along dimension 1, may hold values from -400 to 400
- fir_taps: bfloat16 [64], replicated, may hold values from -0.75 to 0.75
- live_mask: int32 [2560], P(('fibre', 'chan')), parts along dimension 0, may hold values 0 or 1
Outputs:
- correlations: bfloat16 [2560, 256, 256], P(('fibre', 'chan'), 'tm'), parts along dimension 0
There are 2 independent parts, one for each index of `fibre`. A program takes and returns all parts, laid end to end along the dimension named above; an argument that names none is the same for every part. Nothing has to cross between parts.
All inputs are finite; a program needn't handle non-finite values. No bound on the sum of `live_mask` on one device may be relied on, other than what follows from the above.
Results may differ from a plain program's by a relative error of at most 0.0075.
Values may be sent and summed in bfloat16 or wider, within the bound.
A program may use at most 64 MiB of HBM per device.

v0:
```python
import math
import jax
import jax.numpy as jnp
from jax import lax
from jax.sharding import PartitionSpec as P

OFF = 256
LAG = 128
TAPS = 64
STRIDE = 4
REACH = 2
HIST = 60


def shifted(block, axis, distance):
    devices = range(lax.axis_size(axis))
    route = [(i - distance, i) for i in devices if i - distance in devices]
    return lax.ppermute(block, axis, route)


def decimate(tracts, history, fir_taps):
    window_count, channels, tract_len = tracts.shape
    spans = jnp.concatenate([history, tracts], axis=2)
    total_len = spans.shape[2]
    outputs = tract_len // STRIDE
    grouped = spans.reshape(window_count, channels, total_len // STRIDE, STRIDE)
    reversed_taps = fir_taps[::-1]
    filtered = jnp.zeros((window_count, channels, outputs), jnp.float32)
    for block in range(TAPS // STRIDE):
        filtered = filtered + jnp.einsum(
            "wcns,s->wcn",
            grouped[:, :, block : block + outputs, :],
            reversed_taps[block * STRIDE : (block + 1) * STRIDE],
            preferred_element_type=jnp.float32,
        )
    return filtered.astype(jnp.bfloat16)


def whiten(decimated, live_mask):
    values = decimated.astype(jnp.float32)
    loudness = jnp.sqrt(jnp.mean(values * values, axis=2) + 1e-06)
    alive_flags = live_mask.astype(jnp.float32)
    return (values * (alive_flags[None, :, None] / loudness[:, :, None])).astype(jnp.bfloat16)


def correlate(own_block, extended, lag_start, lag_dev):
    window_count, channels, samples = own_block.shape
    group_size = min(8, channels)
    padded_x = jnp.pad(own_block, ((0, 0), (0, 0), (lag_dev, lag_dev)))
    padded_y = jnp.pad(extended, ((0, 0), (0, 0), (LAG, LAG)))
    span_len = samples + lag_dev
    full_len = samples + 2 * lag_dev
    y_window = lax.dynamic_slice_in_dim(padded_y, lag_start, span_len, 2)
    norm_scale = 1.0 / math.sqrt(samples * window_count)
    partner_rows = group_size + OFF - 1

    def one_group(group_index, result):
        first_chan = group_index * group_size
        chosen = lax.dynamic_slice_in_dim(padded_x, first_chan, group_size, 1)
        repeated = jnp.tile(chosen, (1, 1, lag_dev))
        skewed = repeated[:, :, lag_dev : lag_dev + lag_dev * (full_len - 1)]
        toeplitz = skewed.reshape(window_count, group_size, lag_dev, full_len - 1)[
            :, :, :, :span_len
        ]
        partner = lax.dynamic_slice_in_dim(y_window, first_chan + 1, partner_rows, 1)
        lag_sums = jnp.einsum(
            "wglr,wur->glu", toeplitz, partner, preferred_element_type=jnp.float32
        )
        banded = jnp.stack(
            [lag_sums[member, :, member : member + OFF] for member in range(group_size)], axis=0
        )
        return lax.dynamic_update_slice_in_dim(
            result, (banded * norm_scale).astype(jnp.bfloat16), first_chan, 0
        )

    result = jnp.zeros((channels, lag_dev, OFF), jnp.bfloat16)
    return lax.fori_loop(0, channels // group_size, one_group, result)


def shards(raw_strain, fir_taps, live_mask):
    window_count, channels, tract_len = raw_strain.shape
    turned = lax.all_to_all(raw_strain, "chan", split_axis=1, concat_axis=2, tiled=True)
    no_history = jnp.zeros((window_count, turned.shape[1], HIST), jnp.bfloat16)
    decimated = decimate(turned, no_history, fir_taps)
    whitened_here = whiten(decimated, live_mask)
    whitened = lax.all_gather(whitened_here, "tm", axis=0, tiled=True)
    blocks = [whitened]
    for distance in range(1, REACH + 1):
        blocks.append(shifted(whitened, "chan", -distance))
    extended = jnp.concatenate(blocks, axis=1)
    lag_dev = 2 * LAG // lax.axis_size("tm")
    lag_start = lax.axis_index("tm") * lag_dev
    return correlate(whitened, extended, lag_start, lag_dev)


def solution(mesh):
    placed = (P("tm", "fibre", "chan"), P(), P(("fibre", "chan")))
    return jax.shard_map(
        shards,
        mesh=mesh,
        in_specs=placed,
        out_specs=P(("fibre", "chan"), "tm", None),
        check_vma=False,
    )
```

profile of v0, /device:TPU:1, one launch (start us, length us, event | category | flops | bytes accessed | tf_op | source)
XLA Modules:
  0.0 182.1 jit_solution(3668825591206927714)
XLA Ops:
  1.9 7.5 %reduce.2 = bf16[1280,64]{1,0:T(8,128)(2,1)S(1)} reduce(bf16[1280,1,64]{2,1,0:T(2,128)(2,1)S(1)} %bitcast.201, bf16[]{:T(256)} %broadcast.60), dimensions={1}, to_apply=%bitcast.176.reduce_sub_computation | reduce | bytes 327682
  10.2 6.4 %all-to-all-start = ((bf16[8,2,5120]{2,1,0:T(2,128)(2,1)}), bf16[8,2,5120]{2,1,0:T(2,128)(2,1)S(1)}, u32[]{:S(2)}, u32[]{:S(2)}) async-start(bf16[8,2,5120]{2,1,0:T(2,128)(2,1)} %reshape.165), calls=%async_computation | async-start | bytes 327680 | tf_op jit(solution)/shard_map/all_to_all | solution.py:82
  18.3 4.4 %all-to-all-done = bf16[8,2,5120]{2,1,0:T(2,128)(2,1)S(1)} async-done(((bf16[8,2,5120]{2,1,0:T(2,128)(2,1)}), bf16[8,2,5120]{2,1,0:T(2,128)(2,1)S(1)}, u32[]{:S(2)}, u32[]{:S(2)}) %all-to-all-start) | async-done | bytes 163872 | tf_op jit(solution)/shard_map/all_to_all | solution.py:82
  35.4 4.4 %collective-permute-start = (bf16[2,160,128]{2,1,0:T(8,128)(2,1)S(1)}, bf16[2,160,128]{2,1,0:T(8,128)(2,1)S(1)}, u32[]{:S(2)}, u32[]{:S(2)}) collective-permute-start(bf16[2,160,128]{2,1,0:T(8,128)(2,1)S(1)} %bitcast.206), channel_id=1, source_target_pairs={{2,0},{4,2},{6,4},{8,6},{10,8},{12,10},{14,12},{3,1},{5,3},{7,5},{... | collective-permute-start | bytes 245768 | tf_op jit(solution)/shard_map/ppermute | solution.py:18
  39.8 4.1 %collective-permute-done = bf16[2,160,128]{2,1,0:T(8,128)(2,1)S(1)} collective-permute-done((bf16[2,160,128]{2,1,0:T(8,128)(2,1)S(1)}, bf16[2,160,128]{2,1,0:T(8,128)(2,1)S(1)}, u32[]{:S(2)}, u32[]{:S(2)}) %collective-permute-start) | collective-permute-done | bytes 81952 | tf_op jit(solution)/shard_map/ppermute | solution.py:18
  45.1 5.4 %broadcast_in_dim.2.clone = bf16[160,128,256]{2,1,0:T(8,128)(2,1)} broadcast(bf16[]{:T(256)} %constant.76.clone.1), dimensions={} | broadcast | bytes 10485762 | tf_op jit(solution)/shard_map/broadcast_in_dim | solution.py:76
  50.5 131.6 %while.15 = (s32[]{:T(128)}, bf16[160,128,256]{2,1,0:T(8,128)(2,1)}, bf16[2,160,384]{2,1,0:T(8,128)(2,1)S(1)}, bf16[2,480,256]{2,1,0:T(8,128)(2,1)}, s32[]{:T(12...) while((s32[]{:T(128)}, bf16[160,128,256]{2,1,0:T(8,128)(2,1)}, bf16[2,160,384]{2,1,0:T(8,128)(2,1)S(1)}, ...), condition=%wide.region_2.3_spmd, body=%wide.region_1.2_spmd.sunk | while | flops 276299776 | bytes 16048325 | solution.py:77
  50.8 3.5 %reshape.168 = bf16[2,8,128,383]{3,2,1,0:T(8,128)(2,1)S(1)} reshape(bf16[2,8,49024]{2,1,0:T(8,128)(2,1)S(1)} %slice.395) | data formatting | bytes 3137536 | tf_op jit(solution)/shard_map/while/body/eval_jaxpr/reshape | solution.py:62
  57.4 3.5 %reshape.168 = bf16[2,8,128,383]{3,2,1,0:T(8,128)(2,1)S(1)} reshape(bf16[2,8,49024]{2,1,0:T(8,128)(2,1)S(1)} %slice.395) | data formatting | bytes 3137536 | tf_op jit(solution)/shard_map/while/body/eval_jaxpr/reshape | solution.py:62
  64.0 3.5 %reshape.168 = bf16[2,8,128,383]{3,2,1,0:T(8,128)(2,1)S(1)} reshape(bf16[2,8,49024]{2,1,0:T(8,128)(2,1)S(1)} %slice.395) | data formatting | bytes 3137536 | tf_op jit(solution)/shard_map/while/body/eval_jaxpr/reshape | solution.py:62
  70.5 3.5 %reshape.168 = bf16[2,8,128,383]{3,2,1,0:T(8,128)(2,1)S(1)} reshape(bf16[2,8,49024]{2,1,0:T(8,128)(2,1)S(1)} %slice.395) | data formatting | bytes 3137536 | tf_op jit(solution)/shard_map/while/body/eval_jaxpr/reshape | solution.py:62
  77.1 3.5 %reshape.168 = bf16[2,8,128,383]{3,2,1,0:T(8,128)(2,1)S(1)} reshape(bf16[2,8,49024]{2,1,0:T(8,128)(2,1)S(1)} %slice.395) | data formatting | bytes 3137536 | tf_op jit(solution)/shard_map/while/body/eval_jaxpr/reshape | solution.py:62
  83.7 3.5 %reshape.168 = bf16[2,8,128,383]{3,2,1,0:T(8,128)(2,1)S(1)} reshape(bf16[2,8,49024]{2,1,0:T(8,128)(2,1)S(1)} %slice.395) | data formatting | bytes 3137536 | tf_op jit(solution)/shard_map/while/body/eval_jaxpr/reshape | solution.py:62
  90.3 3.5 %reshape.168 = bf16[2,8,128,383]{3,2,1,0:T(8,128)(2,1)S(1)} reshape(bf16[2,8,49024]{2,1,0:T(8,128)(2,1)S(1)} %slice.395) | data formatting | bytes 3137536 | tf_op jit(solution)/shard_map/while/body/eval_jaxpr/reshape | solution.py:62
  96.9 3.5 %reshape.168 = bf16[2,8,128,383]{3,2,1,0:T(8,128)(2,1)S(1)} reshape(bf16[2,8,49024]{2,1,0:T(8,128)(2,1)S(1)} %slice.395) | data formatting | bytes 3137536 | tf_op jit(solution)/shard_map/while/body/eval_jaxpr/reshape | solution.py:62
  110.0 3.5 %reshape.168 = bf16[2,8,128,383]{3,2,1,0:T(8,128)(2,1)S(1)} reshape(bf16[2,8,49024]{2,1,0:T(8,128)(2,1)S(1)} %slice.395) | data formatting | bytes 3137536 | tf_op jit(solution)/shard_map/while/body/eval_jaxpr/reshape | solution.py:62
  116.6 3.5 %reshape.168 = bf16[2,8,128,383]{3,2,1,0:T(8,128)(2,1)S(1)} reshape(bf16[2,8,49024]{2,1,0:T(8,128)(2,1)S(1)} %slice.395) | data formatting | bytes 3137536 | tf_op jit(solution)/shard_map/while/body/eval_jaxpr/reshape | solution.py:62
  123.2 3.5 %reshape.168 = bf16[2,8,128,383]{3,2,1,0:T(8,128)(2,1)S(1)} reshape(bf16[2,8,49024]{2,1,0:T(8,128)(2,1)S(1)} %slice.395) | data formatting | bytes 3137536 | tf_op jit(solution)/shard_map/while/body/eval_jaxpr/reshape | solution.py:62
  129.8 3.5 %reshape.168 = bf16[2,8,128,383]{3,2,1,0:T(8,128)(2,1)S(1)} reshape(bf16[2,8,49024]{2,1,0:T(8,128)(2,1)S(1)} %slice.395) | data formatting | bytes 3137536 | tf_op jit(solution)/shard_map/while/body/eval_jaxpr/reshape | solution.py:62
  142.9 3.5 %reshape.168 = bf16[2,8,128,383]{3,2,1,0:T(8,128)(2,1)S(1)} reshape(bf16[2,8,49024]{2,1,0:T(8,128)(2,1)S(1)} %slice.395) | data formatting | bytes 3137536 | tf_op jit(solution)/shard_map/while/body/eval_jaxpr/reshape | solution.py:62
  149.5 3.5 %reshape.168 = bf16[2,8,128,383]{3,2,1,0:T(8,128)(2,1)S(1)} reshape(bf16[2,8,49024]{2,1,0:T(8,128)(2,1)S(1)} %slice.395) | data formatting | bytes 3137536 | tf_op jit(solution)/shard_map/while/body/eval_jaxpr/reshape | solution.py:62
  162.7 3.5 %reshape.168 = bf16[2,8,128,383]{3,2,1,0:T(8,128)(2,1)S(1)} reshape(bf16[2,8,49024]{2,1,0:T(8,128)(2,1)S(1)} %slice.395) | data formatting | bytes 3137536 | tf_op jit(solution)/shard_map/while/body/eval_jaxpr/reshape | solution.py:62
  169.2 3.5 %reshape.168 = bf16[2,8,128,383]{3,2,1,0:T(8,128)(2,1)S(1)} reshape(bf16[2,8,49024]{2,1,0:T(8,128)(2,1)S(1)} %slice.395) | data formatting | bytes 3137536 | tf_op jit(solution)/shard_map/while/body/eval_jaxpr/reshape | solution.py:62
  175.8 3.5 %reshape.168 = bf16[2,8,128,383]{3,2,1,0:T(8,128)(2,1)S(1)} reshape(bf16[2,8,49024]{2,1,0:T(8,128)(2,1)S(1)} %slice.395) | data formatting | bytes 3137536 | tf_op jit(solution)/shard_map/while/body/eval_jaxpr/reshape | solution.py:62
  (373 shorter events, 87.5 us)
Async XLA Ops:
  0.0 16.6 %copy-start = (bf16[64]{0:T(256)(128)(2,1)S(1)}, bf16[64]{0:T(256)(128)(2,1)}, u32[]{:S(2)}) copy-start(bf16[64]{0:T(256)(128)(2,1)} %param.6) | copy-start | bytes 388
  10.2 12.4 %all-to-all-start = ((bf16[8,2,5120]{2,1,0:T(2,128)(2,1)}), bf16[8,2,5120]{2,1,0:T(2,128)(2,1)S(1)}, u32[]{:S(2)}, u32[]{:S(2)}) async-start(bf16[8,2,5120]{2,1,0:T(2,128)(2,1)} %reshape.165), calls=%async_computation | async-start | bytes 327680 | tf_op jit(solution)/shard_map/all_to_all | solution.py:82
  29.4 1.1 copy-start.1
  34.1 5.7 %collective-permute-start.1 = (bf16[2,160,128]{2,1,0:T(8,128)(2,1)S(1)}, bf16[2,160,128]{2,1,0:T(8,128)(2,1)S(1)}, u32[]{:S(2)}, u32[]{:S(2)}) collective-permute-start(bf16[2,160,128]{2,1,0:T(8,128)(2,1)S(1)} %bitcast.205), channel_id=1, source_target_pairs={{4,0},{6,2},{8,4},{10,6},{12,8},{14,10},{5,1},{7,3},{9,5},{11,7},{... | collective-permute-start | bytes 245768 | tf_op jit(solution)/shard_map/ppermute | solution.py:18
  35.4 8.6 %collective-permute-start = (bf16[2,160,128]{2,1,0:T(8,128)(2,1)S(1)}, bf16[2,160,128]{2,1,0:T(8,128)(2,1)S(1)}, u32[]{:S(2)}, u32[]{:S(2)}) collective-permute-start(bf16[2,160,128]{2,1,0:T(8,128)(2,1)S(1)} %bitcast.206), channel_id=1, source_target_pairs={{2,0},{4,2},{6,4},{8,6},{10,8},{12,10},{14,12},{3,1},{5,3},{7,5},{... | collective-permute-start | bytes 245768 | tf_op jit(solution)/shard_map/ppermute | solution.py:18
where the time goes:
time: 183 us; the launch traced here: 182 us
  local copies, waits for them, and re-layouts  111 us (61%)
  matrix products  33.6 us (18%)
  starting transfers between devices  12 us (7%)
  other arithmetic  10.7 us (6%)
  waiting for transfers between devices  8.51 us (5%)
  blocking collectives  3.52 us (2%)
  loops' own time  2.11 us (1%)
    reshape x20, local copies, waits for them, and re-layouts, one_group(): skewed.reshape(window_count, group_size, lag_dev, full_len - 1)  70.8 us
    dot_general x20, matrix products, one_group(): jnp.einsum('wglr,wur->glu', toeplitz, partner, preferred_element_type=jnp...  29 us
    dynamic_update_slice x40, local copies, waits for them, and re-layouts, one_group(): lax.dynamic_update_slice_in_dim(result, (banded * norm_scale).astype(jnp....  20.9 us
    unnamed x1, other arithmetic  7.45 us
    all_to_all x1, starting transfers between devices, shards(): lax.all_to_all(raw_strain, 'chan', split_axis=1, concat_axis=2, tiled=True)  6.37 us
    ppermute x2, starting transfers between devices, shifted(): return lax.ppermute(block, axis, route)  5.67 us
    broadcast_in_dim x1, local copies, waits for them, and re-layouts, correlate(): result = jnp.zeros((channels, lag_dev, OFF), jnp.bfloat16)  5.4 us
    dot_general x16, matrix products, decimate(): jnp.einsum('wcns,s->wcn', grouped[:, :, block:block + outputs, :], revers...  4.57 us
  transfers between devices with their start and end apart: 3, of which 2 were waited for; matrix products, arithmetic and copies ran while one was open for 1% of the time, Pallas kernels for 0%

commit v1 on v0

--- a/solution.py
+++ b/solution.py
@@ -10,6 +10,17 @@
 STRIDE = 4
 REACH = 2
 HIST = 60
+
+
+def in_blocks(x, dim, size):
+    before, after = (x.shape[:dim], x.shape[dim + 1 :])
+    return jnp.moveaxis(x.reshape(*before, size, -1, *after), dim, 0)
+
+
+def joined_along(pieces, dim):
+    pieces = jnp.moveaxis(pieces, 0, dim)
+    lengths = pieces.shape
+    return pieces.reshape(*lengths[:dim], lengths[dim] * lengths[dim + 1], *lengths[dim + 2 :])
 
 
 def shifted(block, axis, distance):
@@ -79,7 +90,14 @@
 
 def shards(raw_strain, fir_taps, live_mask):
     window_count, channels, tract_len = raw_strain.shape
-    turned = lax.all_to_all(raw_strain, "chan", split_axis=1, concat_axis=2, tiled=True)
+    size, here = (lax.axis_size("chan"), lax.axis_index("chan"))
+    parts = in_blocks(raw_strain, 1, size)
+    finished = [parts[here]]
+    for step in range(1, size):
+        sent = parts[here ^ step]
+        finished.append(lax.ppermute(sent, "chan", [(i_2, i_2 ^ step) for i_2 in range(size)]))
+    parts = jnp.stack(finished)[here ^ jnp.arange(size)]
+    turned = joined_along(parts, 2)
     no_history = jnp.zeros((window_count, turned.shape[1], HIST), jnp.bfloat16)
     decimated = decimate(turned, no_history, fir_taps)
     whitened_here = whiten(decimated, live_mask)

time: 183 us -> 177 us (0.967)
  other arithmetic: 10.7 us -> 3.3 us
  starting transfers between devices: 12 us -> 14.3 us
    ppermute x0 -> x7, starting transfers between devices: none -> 9.55 us  [shards(): lax.ppermute(sent, 'chan', [(i_2, i_2 ^ step) for i_2 in range(size)])]
    unnamed x1 -> x0, other arithmetic: 7.45 us -> none
    all_to_all x1 -> x0, starting transfers between devices: 6.37 us -> none  [shards(): lax.all_to_all(raw_strain, 'chan', split_axis=1, concat_axis=2, tiled=True)]
    ppermute x0 -> x7, waiting for transfers between devices: none -> 4.89 us  [shards(): lax.ppermute(sent, 'chan', [(i_2, i_2 ^ step) for i_2 in range(size)])]
    all_to_all x1 -> x0, waiting for transfers between devices: 4.38 us -> none  [shards(): lax.all_to_all(raw_strain, 'chan', split_axis=1, concat_axis=2, tiled=True)]
    unnamed x9 -> x18, local copies, waits for them, and re-layouts: 3.16 us -> 0.08 us
  transfers between devices with their start and end apart: 3 -> 9, of which waited for: 2 -> 4; matrix products, arithmetic and copies ran while one was open for 1% -> 1% of each run, Pallas kernels for 0% -> 0%
where the time goes in v1:
time: 177 us; the launch traced here: 176 us
  local copies, waits for them, and re-layouts  110 us (62%)
  matrix products  33.6 us (19%)
  starting transfers between devices  14.3 us (8%)
  waiting for transfers between devices  9.21 us (5%)
  blocking collectives  3.52 us (2%)
  other arithmetic  3.3 us (2%)
  loops' own time  2.11 us (1%)
    reshape x20, local copies, waits for them, and re-layouts, one_group(): skewed.reshape(window_count, group_size, lag_dev, full_len - 1)  70.8 us
    dot_general x20, matrix products, one_group(): jnp.einsum('wglr,wur->glu', toeplitz, partner, preferred_element_type=jnp...  29 us
    dynamic_update_slice x40, local copies, waits for them, and re-layouts, one_group(): lax.dynamic_update_slice_in_dim(result, (banded * norm_scale).astype(jnp....  20.9 us
    ppermute x7, starting transfers between devices, shards(): lax.ppermute(sent, 'chan', [(i_2, i_2 ^ step) for i_2 in range(size)])  9.55 us
    broadcast_in_dim x1, local copies, waits for them, and re-layouts, correlate(): result = jnp.zeros((channels, lag_dev, OFF), jnp.bfloat16)  5.4 us
    ppermute x7, waiting for transfers between devices, shards(): lax.ppermute(sent, 'chan', [(i_2, i_2 ^ step) for i_2 in range(size)])  4.89 us
    ppermute x2, starting transfers between devices, shifted(): return lax.ppermute(block, axis, route)  4.7 us
    dot_general x16, matrix products, decimate(): jnp.einsum('wcns,s->wcn', grouped[:, :, block:block + outputs, :], revers...  4.57 us
  transfers between devices with their start and end apart: 9, of which 4 were waited for; matrix products, arithmetic and copies ran while one was open for 1% of the time, Pallas kernels for 0%

profile of v1, /device:TPU:1, one launch (start us, length us, event | category | flops | bytes accessed | tf_op | source)
XLA Modules:
  0.0 176.4 jit_solution(3591019086870613504)
XLA Ops:
  14.5 3.8 %collective-permute-done.6 = bf16[1,160,64]{1,2,0:T(8,128)(2,1)S(1)} collective-permute-done((bf16[1,160,64]{1,2,0:T(8,128)(2,1)S(1)}, bf16[1,160,64]{1,2,0:T(8,128)(2,1)S(1)}, u32[]{:S(2)}, u32[]{:S(2)}) %collective-permute-start.6) | collective-permute-done | bytes 20512 | tf_op jit(solution)/shard_map/ppermute | solution.py:98
  34.3 3.9 %collective-permute-done.7 = bf16[2,160,128]{2,1,0:T(8,128)(2,1)S(1)} collective-permute-done((bf16[2,160,128]{2,1,0:T(8,128)(2,1)S(1)}, bf16[2,160,128]{2,1,0:T(8,128)(2,1)S(1)}, u32[]{:S(2)}, u32[]{:S(2)}) %collective-permute-start.7) | collective-permute-done | bytes 81952 | tf_op jit(solution)/shard_map/ppermute | solution.py:29
  39.4 5.4 %broadcast_in_dim.2.clone = bf16[160,128,256]{2,1,0:T(8,128)(2,1)} broadcast(bf16[]{:T(256)} %constant.89.clone.1), dimensions={} | broadcast | bytes 10485762 | tf_op jit(solution)/shard_map/broadcast_in_dim | solution.py:87
  44.8 131.6 %while.15 = (s32[]{:T(128)}, bf16[160,128,256]{2,1,0:T(8,128)(2,1)}, bf16[2,160,384]{2,1,0:T(8,128)(2,1)S(1)}, bf16[2,480,256]{2,1,0:T(8,128)(2,1)}, s32[]{:T(12...) while((s32[]{:T(128)}, bf16[160,128,256]{2,1,0:T(8,128)(2,1)}, bf16[2,160,384]{2,1,0:T(8,128)(2,1)S(1)}, ...), condition=%wide.region_2.3_spmd, body=%wide.region_1.2_spmd.sunk | while | flops 276299776 | bytes 16048325 | solution.py:88
  45.0 3.5 %reshape.196 = bf16[2,8,128,383]{3,2,1,0:T(8,128)(2,1)S(1)} reshape(bf16[2,8,49024]{2,1,0:T(8,128)(2,1)S(1)} %slice.397) | data formatting | bytes 3137536 | tf_op jit(solution)/shard_map/while/body/eval_jaxpr/reshape | solution.py:73
  51.6 3.5 %reshape.196 = bf16[2,8,128,383]{3,2,1,0:T(8,128)(2,1)S(1)} reshape(bf16[2,8,49024]{2,1,0:T(8,128)(2,1)S(1)} %slice.397) | data formatting | bytes 3137536 | tf_op jit(solution)/shard_map/while/body/eval_jaxpr/reshape | solution.py:73
  58.2 3.5 %reshape.196 = bf16[2,8,128,383]{3,2,1,0:T(8,128)(2,1)S(1)} reshape(bf16[2,8,49024]{2,1,0:T(8,128)(2,1)S(1)} %slice.397) | data formatting | bytes 3137536 | tf_op jit(solution)/shard_map/while/body/eval_jaxpr/reshape | solution.py:73
  64.8 3.5 %reshape.196 = bf16[2,8,128,383]{3,2,1,0:T(8,128)(2,1)S(1)} reshape(bf16[2,8,49024]{2,1,0:T(8,128)(2,1)S(1)} %slice.397) | data formatting | bytes 3137536 | tf_op jit(solution)/shard_map/while/body/eval_jaxpr/reshape | solution.py:73
  71.3 3.5 %reshape.196 = bf16[2,8,128,383]{3,2,1,0:T(8,128)(2,1)S(1)} reshape(bf16[2,8,49024]{2,1,0:T(8,128)(2,1)S(1)} %slice.397) | data formatting | bytes 3137536 | tf_op jit(solution)/shard_map/while/body/eval_jaxpr/reshape | solution.py:73
  77.9 3.5 %reshape.196 = bf16[2,8,128,383]{3,2,1,0:T(8,128)(2,1)S(1)} reshape(bf16[2,8,49024]{2,1,0:T(8,128)(2,1)S(1)} %slice.397) | data formatting | bytes 3137536 | tf_op jit(solution)/shard_map/while/body/eval_jaxpr/reshape | solution.py:73
  84.5 3.5 %reshape.196 = bf16[2,8,128,383]{3,2,1,0:T(8,128)(2,1)S(1)} reshape(bf16[2,8,49024]{2,1,0:T(8,128)(2,1)S(1)} %slice.397) | data formatting | bytes 3137536 | tf_op jit(solution)/shard_map/while/body/eval_jaxpr/reshape | solution.py:73
  91.1 3.5 %reshape.196 = bf16[2,8,128,383]{3,2,1,0:T(8,128)(2,1)S(1)} reshape(bf16[2,8,49024]{2,1,0:T(8,128)(2,1)S(1)} %slice.397) | data formatting | bytes 3137536 | tf_op jit(solution)/shard_map/while/body/eval_jaxpr/reshape | solution.py:73
  97.7 3.5 %reshape.196 = bf16[2,8,128,383]{3,2,1,0:T(8,128)(2,1)S(1)} reshape(bf16[2,8,49024]{2,1,0:T(8,128)(2,1)S(1)} %slice.397) | data formatting | bytes 3137536 | tf_op jit(solution)/shard_map/while/body/eval_jaxpr/reshape | solution.py:73
  104.2 3.5 %reshape.196 = bf16[2,8,128,383]{3,2,1,0:T(8,128)(2,1)S(1)} reshape(bf16[2,8,49024]{2,1,0:T(8,128)(2,1)S(1)} %slice.397) | data formatting | bytes 3137536 | tf_op jit(solution)/shard_map/while/body/eval_jaxpr/reshape | solution.py:73
  110.8 3.5 %reshape.196 = bf16[2,8,128,383]{3,2,1,0:T(8,128)(2,1)S(1)} reshape(bf16[2,8,49024]{2,1,0:T(8,128)(2,1)S(1)} %slice.397) | data formatting | bytes 3137536 | tf_op jit(solution)/shard_map/while/body/eval_jaxpr/reshape | solution.py:73
  117.4 3.5 %reshape.196 = bf16[2,8,128,383]{3,2,1,0:T(8,128)(2,1)S(1)} reshape(bf16[2,8,49024]{2,1,0:T(8,128)(2,1)S(1)} %slice.397) | data formatting | bytes 3137536 | tf_op jit(solution)/shard_map/while/body/eval_jaxpr/reshape | solution.py:73
  124.0 3.5 %reshape.196 = bf16[2,8,128,383]{3,2,1,0:T(8,128)(2,1)S(1)} reshape(bf16[2,8,49024]{2,1,0:T(8,128)(2,1)S(1)} %slice.397) | data formatting | bytes 3137536 | tf_op jit(solution)/shard_map/while/body/eval_jaxpr/reshape | solution.py:73
  130.6 3.5 %reshape.196 = bf16[2,8,128,383]{3,2,1,0:T(8,128)(2,1)S(1)} reshape(bf16[2,8,49024]{2,1,0:T(8,128)(2,1)S(1)} %slice.397) | data formatting | bytes 3137536 | tf_op jit(solution)/shard_map/while/body/eval_jaxpr/reshape | solution.py:73
  137.1 3.5 %reshape.196 = bf16[2,8,128,383]{3,2,1,0:T(8,128)(2,1)S(1)} reshape(bf16[2,8,49024]{2,1,0:T(8,128)(2,1)S(1)} %slice.397) | data formatting | bytes 3137536 | tf_op jit(solution)/shard_map/while/body/eval_jaxpr/reshape | solution.py:73
  143.7 3.5 %reshape.196 = bf16[2,8,128,383]{3,2,1,0:T(8,128)(2,1)S(1)} reshape(bf16[2,8,49024]{2,1,0:T(8,128)(2,1)S(1)} %slice.397) | data formatting | bytes 3137536 | tf_op jit(solution)/shard_map/while/body/eval_jaxpr/reshape | solution.py:73
  150.3 3.5 %reshape.196 = bf16[2,8,128,383]{3,2,1,0:T(8,128)(2,1)S(1)} reshape(bf16[2,8,49024]{2,1,0:T(8,128)(2,1)S(1)} %slice.397) | data formatting | bytes 3137536 | tf_op jit(solution)/shard_map/while/body/eval_jaxpr/reshape | solution.py:73
  156.9 3.5 %reshape.196 = bf16[2,8,128,383]{3,2,1,0:T(8,128)(2,1)S(1)} reshape(bf16[2,8,49024]{2,1,0:T(8,128)(2,1)S(1)} %slice.397) | data formatting | bytes 3137536 | tf_op jit(solution)/shard_map/while/body/eval_jaxpr/reshape | solution.py:73
  163.5 3.5 %reshape.196 = bf16[2,8,128,383]{3,2,1,0:T(8,128)(2,1)S(1)} reshape(bf16[2,8,49024]{2,1,0:T(8,128)(2,1)S(1)} %slice.397) | data formatting | bytes 3137536 | tf_op jit(solution)/shard_map/while/body/eval_jaxpr/reshape | solution.py:73
  170.0 3.5 %reshape.196 = bf16[2,8,128,383]{3,2,1,0:T(8,128)(2,1)S(1)} reshape(bf16[2,8,49024]{2,1,0:T(8,128)(2,1)S(1)} %slice.397) | data formatting | bytes 3137536 | tf_op jit(solution)/shard_map/while/body/eval_jaxpr/reshape | solution.py:73
  (397 shorter events, 90.1 us)
Async XLA Ops:
  0.0 7.9 %copy-start = (bf16[64]{0:T(256)(128)(2,1)S(1)}, bf16[64]{0:T(256)(128)(2,1)}, u32[]{:S(2)}) copy-start(bf16[64]{0:T(256)(128)(2,1)} %param.6) | copy-start | bytes 388
  2.0 7.6 %collective-permute-start = (bf16[1,160,64]{1,2,0:T(8,128)(2,1)S(1)}, bf16[1,160,64]{1,2,0:T(8,128)(2,1)S(1)}, u32[]{:S(2)}, u32[]{:S(2)}) collective-permute-start(bf16[1,160,64]{1,2,0:T(8,128)(2,1)S(1)} %bitcast.264), channel_id=1, source_target_pairs={{0,2},{2,0},{4,6},{6,4},{8,10},{10,8},{12,14},{14,12},{1,3},{3,1},... | collective-permute-start | bytes 61448 | tf_op jit(solution)/shard_map/ppermute | solution.py:98
  2.0 11.0 %collective-permute-start.1 = (bf16[1,160,64]{1,2,0:T(8,128)(2,1)S(1)}, bf16[1,160,64]{1,2,0:T(8,128)(2,1)S(1)}, u32[]{:S(2)}, u32[]{:S(2)}) collective-permute-start(bf16[1,160,64]{1,2,0:T(8,128)(2,1)S(1)} %bitcast.263), channel_id=1, source_target_pairs={{0,4},{2,6},{4,0},{6,2},{8,12},{10,14},{12,8},{14,10},{1,5},{3,7},... | collective-permute-start | bytes 61448 | tf_op jit(solution)/shard_map/ppermute | solution.py:98
  4.8 8.5 %collective-permute-start.2 = (bf16[1,160,64]{1,2,0:T(8,128)(2,1)S(1)}, bf16[1,160,64]{1,2,0:T(8,128)(2,1)S(1)}, u32[]{:S(2)}, u32[]{:S(2)}) collective-permute-start(bf16[1,160,64]{1,2,0:T(8,128)(2,1)S(1)} %bitcast.262), channel_id=1, source_target_pairs={{0,6},{2,4},{4,2},{6,0},{8,14},{10,12},{12,10},{14,8},{1,7},{3,5},... | collective-permute-start | bytes 61448 | tf_op jit(solution)/shard_map/ppermute | solution.py:98
  4.9 8.4 %collective-permute-start.3 = (bf16[1,160,64]{1,2,0:T(8,128)(2,1)S(1)}, bf16[1,160,64]{1,2,0:T(8,128)(2,1)S(1)}, u32[]{:S(2)}, u32[]{:S(2)}) collective-permute-start(bf16[1,160,64]{1,2,0:T(8,128)(2,1)S(1)} %bitcast.261), channel_id=1, source_target_pairs={{0,8},{2,10},{4,12},{6,14},{8,0},{10,2},{12,4},{14,6},{1,9},{3,11}... | collective-permute-start | bytes 61448 | tf_op jit(solution)/shard_map/ppermute | solution.py:98
  7.6 5.8 %collective-permute-start.4 = (bf16[1,160,64]{1,2,0:T(8,128)(2,1)S(1)}, bf16[1,160,64]{1,2,0:T(8,128)(2,1)S(1)}, u32[]{:S(2)}, u32[]{:S(2)}) collective-permute-start(bf16[1,160,64]{1,2,0:T(8,128)(2,1)S(1)} %bitcast.260), channel_id=1, source_target_pairs={{0,10},{2,8},{4,14},{6,12},{8,2},{10,0},{12,6},{14,4},{1,11},{3,9}... | collective-permute-start | bytes 61448 | tf_op jit(solution)/shard_map/ppermute | solution.py:98
  9.6 4.9 %collective-permute-start.5 = (bf16[1,160,64]{1,2,0:T(8,128)(2,1)S(1)}, bf16[1,160,64]{1,2,0:T(8,128)(2,1)S(1)}, u32[]{:S(2)}, u32[]{:S(2)}) collective-permute-start(bf16[1,160,64]{1,2,0:T(8,128)(2,1)S(1)} %bitcast.266), channel_id=1, source_target_pairs={{0,12},{2,14},{4,8},{6,10},{8,4},{10,6},{12,0},{14,2},{1,13},{3,15... | collective-permute-start | bytes 61448 | tf_op jit(solution)/shard_map/ppermute | solution.py:98
  13.1 5.2 %collective-permute-start.6 = (bf16[1,160,64]{1,2,0:T(8,128)(2,1)S(1)}, bf16[1,160,64]{1,2,0:T(8,128)(2,1)S(1)}, u32[]{:S(2)}, u32[]{:S(2)}) collective-permute-start(bf16[1,160,64]{1,2,0:T(8,128)(2,1)S(1)} %bitcast.265), channel_id=1, source_target_pairs={{0,14},{2,12},{4,10},{6,8},{8,6},{10,4},{12,2},{14,0},{1,15},{3,13... | collective-permute-start | bytes 61448 | tf_op jit(solution)/shard_map/ppermute | solution.py:98
  24.4 1.1 copy-start.1
  29.1 5.2 %collective-permute-start.8 = (bf16[2,160,128]{2,1,0:T(8,128)(2,1)S(1)}, bf16[2,160,128]{2,1,0:T(8,128)(2,1)S(1)}, u32[]{:S(2)}, u32[]{:S(2)}) collective-permute-start(bf16[2,160,128]{2,1,0:T(8,128)(2,1)S(1)} %bitcast.255), channel_id=1, source_target_pairs={{4,0},{6,2},{8,4},{10,6},{12,8},{14,10},{5,1},{7,3},{9,5},{11,7},{... | collective-permute-start | bytes 245768 | tf_op jit(solution)/shard_map/ppermute | solution.py:29
  30.4 7.8 %collective-permute-start.7 = (bf16[2,160,128]{2,1,0:T(8,128)(2,1)S(1)}, bf16[2,160,128]{2,1,0:T(8,128)(2,1)S(1)}, u32[]{:S(2)}, u32[]{:S(2)}) collective-permute-start(bf16[2,160,128]{2,1,0:T(8,128)(2,1)S(1)} %bitcast.256), channel_id=1, source_target_pairs={{2,0},{4,2},{6,4},{8,6},{10,8},{12,10},{14,12},{3,1},{5,3},{7,5},{... | collective-permute-start | bytes 245768 | tf_op jit(solution)/shard_map/ppermute | solution.py:29
